TPU v7x, 32 devices: a whole 2x2x4 slice. The times are simulated.
32 devices in a mesh: energy: 8 (over z, y), space: 4 (over x, core).
Axes of the slice: x: 2, y: 2, z: 4, core: 2. Of those that a mesh axis runs over, the one named last changes fastest.
Arguments:
- lesser: bfloat16 [2, 512, 4, 65536], P(None, 'energy', 'space'), may hold values from -6 to 6
- greater: bfloat16 [2, 512, 4, 65536], P(None, 'energy', 'space'), may hold values from -6 to 6
- vdiag: bfloat16 [4, 256, 256], P('space'), may hold values from -0.375 to 0.375
- vlower: bfloat16 [4, 256, 256], P('space'), may hold values from -0.375 to 0.375
- occupancy: int32 [4, 8], P('space'), may hold values from 1 to 32, 128 in all within a row
- tile_order: int32 [4, 512], P('space'), may hold values from 0 to 511, each once within a row
Outputs:
- interaction_diag: bfloat16 [2, 512, 4, 256, 256], P(None, 'energy', 'space')
- interaction_lower: bfloat16 [2, 512, 4, 256, 256], P(None, 'energy', 'space')
Inputs may be any that keep to these rules, and one draw needn't show every extreme that they name: `occupancy`: for each block, the entries sum to 128 and the largest is exactly 32. `tile_order`: each row is a permutation of the tile numbers.
All inputs are finite; a program needn't handle non-finite values.
Results may differ from a plain program's by a relative error of at most 0.015.
Values may be sent and summed in bfloat16 or wider, within the bound.
A program may use at most 448 MiB of HBM per device.

v0:
```python
import jax
import jax.numpy as jnp
from jax import lax
from jax.sharding import PartitionSpec as P

TILE = 128
NNZ = 128


def passed_along(value, axis, steps):
    count = lax.axis_size(axis)
    leading, last = (max(0, -steps), min(count, count - steps))
    return lax.ppermute(value, axis, [(source, source + steps) for source in range(leading, last)])


def split_table(table):
    upper = table.astype(jnp.bfloat16)
    rest = (table - upper.astype(jnp.float32)).astype(jnp.bfloat16)
    return (upper, rest)


def table_times(parts, data):
    first = jnp.dot(parts[0], data, preferred_element_type=jnp.float32)
    return first + jnp.dot(parts[1], data, preferred_element_type=jnp.float32)


def split_times(parts, data):
    upper, rest = split_table(data)
    total = jnp.dot(parts[0], upper, preferred_element_type=jnp.float32)
    total = total + jnp.dot(parts[0], rest, preferred_element_type=jnp.float32)
    return total + jnp.dot(parts[1], upper, preferred_element_type=jnp.float32)


def unpack_tiles(tiles, index, local_energies, n_tiles, width):
    field = jnp.zeros((2, local_energies, n_tiles + 1, tiles.shape[-1]), jnp.bfloat16)
    field = field.at[:, :, index, :].set(tiles)
    return field[:, :, :n_tiles, :].reshape(2, local_energies, width, width)


def per_device(lesser, greater, vdiag, vlower, occupancy, tile_order):
    group_size = lax.axis_size("energy")
    local_energies = lesser.shape[1]
    width = vdiag.shape[1]
    n_tiles = lesser.shape[3] // TILE
    most_tiles = 2 * NNZ // group_size
    counts = occupancy[0]
    tile_perm = tile_order[0]
    slot_ids = jnp.arange(most_tiles, dtype=jnp.int32)
    flat_slot = jnp.arange(group_size, dtype=jnp.int32)[:, None] * most_tiles + slot_ids[None, :]
    listing = jnp.where(slot_ids[None, :] < counts[:, None], tile_perm[flat_slot], n_tiles)
    slot_index = listing.reshape(-1)

    def pack(source):
        tiled = source.reshape(2, local_energies, n_tiles, TILE)
        padded = jnp.concatenate(
            [tiled, jnp.zeros((2, local_energies, 1, TILE), source.dtype)], axis=2
        )
        taken = jnp.take(padded, slot_index, axis=2)
        return taken.reshape(2, local_energies, group_size, most_tiles, TILE)

    lesser_got, greater_got = (
        lax.all_to_all(pack(lesser), "energy", split_axis=2, concat_axis=1, tiled=True),
        lax.all_to_all(pack(greater), "energy", split_axis=2, concat_axis=1, tiled=True),
    )
    energies = local_energies * group_size
    columns = most_tiles * TILE
    lesser_cols = lesser_got.reshape(2, energies, columns)
    greater_cols = greater_got.reshape(2, energies, columns)
    grid = jnp.arange(energies, dtype=jnp.int32)
    phase = (grid[:, None] * grid[None, :] % energies).astype(jnp.float32) * (
        2.0 * jnp.pi / energies
    )
    cos_parts = split_table(jnp.cos(phase))
    sin_parts = split_table(jnp.sin(phase))
    first_real = table_times(cos_parts, lesser_cols[0]) + table_times(sin_parts, lesser_cols[1])
    first_imag = table_times(cos_parts, lesser_cols[1]) - table_times(sin_parts, lesser_cols[0])
    second_real = table_times(cos_parts, greater_cols[0]) - table_times(sin_parts, greater_cols[1])
    second_imag = table_times(cos_parts, greater_cols[1]) + table_times(sin_parts, greater_cols[0])
    product_real = first_real * second_real - first_imag * second_imag
    product_imag = first_real * second_imag + first_imag * second_real
    stacked = jnp.concatenate([product_real, product_imag], axis=1)
    cos_side = split_times(cos_parts, stacked)
    sin_side = split_times(sin_parts, stacked)
    factor = float(energies) ** (-1.5)
    polar_real = factor * (cos_side[:, :columns] - sin_side[:, columns:])
    polar_imag = factor * (cos_side[:, columns:] + sin_side[:, :columns])
    polar_tiles = jnp.stack([polar_real, polar_imag]).astype(jnp.bfloat16)
    polar_tiles = polar_tiles.reshape(2, group_size, local_energies, 1, most_tiles, TILE)
    returned = lax.all_to_all(polar_tiles, "energy", split_axis=1, concat_axis=3, tiled=True)
    returned = returned.reshape(2, local_energies, group_size * most_tiles, TILE)
    own_block = unpack_tiles(returned, slot_index, local_energies, n_tiles, width)
    diag_here = vdiag[0]
    lower_here = vlower[0]
    below_polar, below_diag = passed_along((own_block, diag_here), "space", 1)
    above_polar, above_lower = passed_along((own_block, lower_here), "space", -1)
    left_prod = jnp.einsum(
        "ab,xebc->xeac", lower_here, below_polar, preferred_element_type=jnp.float32
    ).astype(jnp.bfloat16)
    middle_prod = jnp.einsum(
        "ab,xebc->xeac", diag_here, own_block, preferred_element_type=jnp.float32
    ).astype(jnp.bfloat16)
    right_prod = jnp.einsum(
        "ba,xebc->xeac", above_lower, above_polar, preferred_element_type=jnp.float32
    ).astype(jnp.bfloat16)
    diag_sum = jnp.einsum(
        "xeab,cb->xeac", left_prod, lower_here, preferred_element_type=jnp.float32
    )
    diag_sum = diag_sum + jnp.einsum(
        "xeab,bc->xeac", middle_prod, diag_here, preferred_element_type=jnp.float32
    )
    diag_sum = diag_sum + jnp.einsum(
        "xeab,bc->xeac", right_prod, above_lower, preferred_element_type=jnp.float32
    )
    lower_sum = jnp.einsum(
        "xeab,bc->xeac", left_prod, below_diag, preferred_element_type=jnp.float32
    )
    lower_sum = lower_sum + jnp.einsum(
        "xeab,cb->xeac", middle_prod, lower_here, preferred_element_type=jnp.float32
    )
    diag_out = diag_sum.astype(jnp.bfloat16).reshape(2, local_energies, 1, width, width)
    lower_out = lower_sum.astype(jnp.bfloat16).reshape(2, local_energies, 1, width, width)
    return (diag_out, lower_out)


def solution(mesh):
    return jax.shard_map(
        per_device,
        mesh=mesh,
        in_specs=(
            P(None, "energy", "space", None),
            P(None, "energy", "space", None),
            P("space", None, None),
            P("space", None, None),
            P("space", None),
            P("space", None),
        ),
        out_specs=(P(None, "energy", "space", None, None), P(None, "energy", "space", None, None)),
        check_vma=False,
    )
```

profile of v0, /device:TPU:1, one launch (start us, length us, event | category | flops | bytes accessed | tf_op | source)
XLA Modules:
  0.0 1499.1 jit_solution(4860167797015654437)
XLA Ops:
  4.2 9.7 copy.89
  13.9 37.2 %copy.60 = bf16[2,64,512,128]{3,1,2,0:T(8,128)(2,1)S(1)} copy(bf16[2,64,512,128]{3,2,1,0:T(8,128)(2,1)S(1)} %bitcast.170) | data formatting | bytes 33554432 | tf_op jit(solution)/shard_map/reshape | solution.py:54
  51.1 9.7 copy.92
  60.8 40.3 %copy.62 = bf16[2,64,512,128]{3,1,2,0:T(8,128)(2,1)} copy(bf16[2,64,512,128]{3,2,1,0:T(8,128)(2,1)S(1)} %bitcast.171) | data formatting | bytes 33554432 | tf_op jit(solution)/shard_map/reshape | solution.py:54
  101.1 9.1 concatenate.17
  121.1 14.4 gather_fusion.1
  135.5 14.9 gather_fusion.2
  150.4 11.9 broadcast_select_fusion
  162.3 13.7 copy.63
  182.6 13.8 copy.61
  196.4 168.3 %all-to-all-done.1 = bf16[2,64,8,32,128]{4,3,1,0,2:T(8,128)(2,1)} async-done(((bf16[2,64,8,32,128]{4,3,1,0,2:T(8,128)(2,1)}), bf16[2,64,8,32,128]{4,3,1,0,2:T(8,128)(2,1)}, u32[]{:S(2)}, u32[]{:S(2)}) %all-to-all-start.1) | async-done | bytes 8388640 | tf_op jit(solution)/shard_map/all_to_all | solution.py:63
  384.4 8.9 fusion.34
  393.3 157.9 %all-to-all-done = bf16[2,64,8,32,128]{4,3,1,0,2:T(8,128)(2,1)} async-done(((bf16[2,64,8,32,128]{4,3,1,0,2:T(8,128)(2,1)}), bf16[2,64,8,32,128]{4,3,1,0,2:T(8,128)(2,1)}, u32[]{:S(2)}, u32[]{:S(2)}) %all-to-all-start) | async-done | bytes 8388640 | tf_op jit(solution)/shard_map/all_to_all | solution.py:62
  555.4 9.3 fusion.48
  564.8 8.9 fusion.50
  573.7 9.1 fusion.29
  582.7 9.2 fusion.24
  592.0 9.0 fusion.26
  601.0 9.0 fusion.32
  610.0 9.1 fusion.43
  628.0 8.9 fusion.40
  636.9 9.3 fusion.46
  646.3 15.4 %add_subtract_fusion.1 = f32[512,4096]{1,0:T(8,128)S(1)} fusion(f32[512,4096]{1,0:T(8,128)} %fusion.29, f32[512,4096]{1,0:T(8,128)} %fusion.36, f32[512,4096]{1,0:T(8,128)} %fusion.34, bf16[64,8,32,128]{3,2,1,0:T(8,128)(2,1)} %bitcast.185), kind=kOutput, calls=%fused_computation.36 | convolution fusion | flops 2158493696 | bytes 37748736 | tf_op jit(solution)/shard_map/dot_general | solution.py:24
  661.7 18.6 %add_add_fusion.3 = f32[512,4096]{1,0:T(8,128)} fusion(f32[512,4096]{1,0:T(8,128)} %fusion.43, f32[512,4096]{1,0:T(8,128)} %fusion.50, f32[512,4096]{1,0:T(8,128)} %fusion.48, bf16[64,8,32,128]{3,2,1,0:T(8,128)(2,1)} %bitcast.192), kind=kOutput, calls=%fused_computation.37 | convolution fusion | flops 2158493696 | bytes 37748736 | tf_op jit(solution)/shard_map/dot_general | solution.py:24
  680.3 15.8 %add_add_fusion.2 = f32[512,4096]{1,0:T(8,128)} fusion(f32[512,4096]{1,0:T(8,128)} %fusion.32, f32[512,4096]{1,0:T(8,128)} %fusion.26, f32[512,4096]{1,0:T(8,128)} %fusion.24, bf16[64,8,32,128]{3,2,1,0:T(8,128)(2,1)S(1)} %bitcast.180), kind=kOutput, calls=%fused_computation.34 | convolution fusion | flops 2158493696 | bytes 37748736 | tf_op jit(solution)/shard_map/dot_general | solution.py:24
  696.1 25.4 %multiply_subtract_fusion = (f32[512,4096]{1,0:T(8,128)}, f32[512,4096]{1,0:T(8,128)}) fusion(f32[512,4096]{1,0:T(8,128)} %add_add_fusion.2, f32[512,4096]{1,0:T(8,128)} %add_add_fusion.3, f32[512,4096]{1,0:T(8,128)S(1)} %add_subtract_fusion.1, f32[512,4096]{1,0:T(8,128)} %fusion.46, bf16[64,8,32,128]{3,2,1,0:T(8,128)(2,1)} %bitcast.184, ...), kind=kOutput, calls=%fused_computation.33 | convolution fusion | flops 2171076608 | bytes 71303168 | tf_op jit(solution)/shard_map/dot_general | solution.py:24
  721.5 19.7 %fusion.77 = f32[512,8192]{1,0:T(8,128)} fusion(f32[512,4096]{1,0:T(8,128)} %get-tuple-element.16, f32[512,4096]{1,0:T(8,128)} %get-tuple-element.15), kind=kOutput, calls=%fused_computation.100 | convolution fusion | flops 4319870976 | bytes 33554432 | tf_op jit(solution)/shard_map/dot_general | solution.py:30
  741.2 20.0 %fusion.79 = f32[512,8192]{1,0:T(8,128)} fusion(f32[512,4096]{1,0:T(8,128)} %get-tuple-element.16, f32[512,4096]{1,0:T(8,128)} %get-tuple-element.15), kind=kOutput, calls=%fused_computation.101 | convolution fusion | flops 4315676672 | bytes 33554432 | tf_op jit(solution)/shard_map/dot_general | solution.py:29
  761.2 20.1 %fusion.86 = f32[512,8192]{1,0:T(8,128)} fusion(f32[512,4096]{1,0:T(8,128)} %get-tuple-element.16, f32[512,4096]{1,0:T(8,128)} %get-tuple-element.15), kind=kOutput, calls=%fused_computation.103 | convolution fusion | flops 4319870976 | bytes 33554432 | tf_op jit(solution)/shard_map/dot_general | solution.py:30
  781.4 20.2 %fusion.88 = f32[512,8192]{1,0:T(8,128)} fusion(f32[512,4096]{1,0:T(8,128)} %get-tuple-element.16, f32[512,4096]{1,0:T(8,128)} %get-tuple-element.15), kind=kOutput, calls=%fused_computation.104 | convolution fusion | flops 4315676672 | bytes 33554432 | tf_op jit(solution)/shard_map/dot_general | solution.py:29
  801.6 23.7 %add_add_fusion.1 = f32[512,8192]{1,0:T(8,128)} fusion(f32[512,8192]{1,0:T(8,128)} %fusion.79, f32[512,8192]{1,0:T(8,128)} %fusion.77, f32[512,4096]{1,0:T(8,128)} %get-tuple-element.16, f32[512,4096]{1,0:T(8,128)} %get-tuple-element.15), kind=kOutput, calls=%fused_computation.17 | convolution fusion | flops 4324851712 | bytes 67108864 | tf_op jit(solution)/shard_map/dot_general | solution.py:31
  825.3 23.7 %add_add_fusion = f32[512,8192]{1,0:T(8,128)} fusion(f32[512,8192]{1,0:T(8,128)} %fusion.88, f32[512,8192]{1,0:T(8,128)} %fusion.86, f32[512,4096]{1,0:T(8,128)} %get-tuple-element.16, f32[512,4096]{1,0:T(8,128)} %get-tuple-element.15), kind=kOutput, calls=%fused_computation.16 | convolution fusion | flops 4324851712 | bytes 67108864 | tf_op jit(solution)/shard_map/dot_general | solution.py:31
  849.1 12.9 fusion.22
  880.8 181.1 %all-to-all-done.2 = bf16[2,8,64,1,32,128]{5,4,2,3,0,1:T(8,128)(2,1)} async-done(((bf16[2,8,64,1,32,128]{5,4,2,3,0,1:T(8,128)(2,1)}), bf16[2,8,64,1,32,128]{5,4,2,3,0,1:T(8,128)(2,1)}, u32[]{:S(2)}, u32[]{:S(2)}) %all-to-all-start.2) | async-done | bytes 8388640 | tf_op jit(solution)/shard_map/all_to_all | solution.py:89
  1061.9 9.4 copy.66
  1071.3 12.2 copy.67
  1089.5 41.1 %scatter_fusion = bf16[2,64,513,128]{3,1,2,0:T(8,128)(2,1)} fusion(bf16[2,64,513,128]{3,1,2,0:T(8,128)(2,1)} %broadcast_in_dim.13, s32[256]{0:T(256)S(1)} %bitcast.197, bf16[256,2,64,128]{3,2,1,0:T(8,128)(2,1)} %copy.67), kind=kCustom, calls=%fused_computation.3 | custom fusion | bytes 25166848 | tf_op jit(solution)/shard_map/scatter | solution.py:36
  1138.7 36.2 %copy.68 = bf16[2,64,512,128]{3,2,1,0:T(8,128)(2,1)} copy(bf16[2,64,512,128]{3,1,2,0:T(8,128)(2,1)S(1)} %slice.58) | data formatting | bytes 33554432 | tf_op jit(solution)/shard_map/slice | solution.py:37
  1174.9 24.4 %reshape.176 = bf16[2,64,256,256]{3,2,1,0:T(8,128)(2,1)} reshape(bf16[2,64,512,128]{3,2,1,0:T(8,128)(2,1)} %copy.68) | data formatting | bytes 33554432 | tf_op jit(solution)/shard_map/reshape | solution.py:37
  1199.3 21.2 %copy.69 = bf16[2,64,256,256]{2,3,1,0:T(8,128)(2,1)} copy(bf16[2,64,256,256]{3,2,1,0:T(8,128)(2,1)} %reshape.176) | data formatting | bytes 33554432 | tf_op jit(solution)/shard_map/reshape | solution.py:37
  1237.0 12.1 convolution_convert_fusion
  1249.1 21.4 %fusion.1 = f32[2,64,256,256]{3,2,1,0:T(8,128)} fusion(bf16[2,64,256,256]{3,2,1,0:T(8,128)(2,1)} %convolution_convert_fusion, bf16[1,256,256]{2,1,0:T(8,128)(2,1)S(1)} %copy-done.9), kind=kOutput, calls=%fused_computation.8 | convolution fusion | flops 4294967296 | bytes 50462720 | tf_op jit(solution)/shard_map/xeab,cb->xeac/dot_general | solution.py:117
  1270.6 21.4 %fusion.3 = f32[2,64,256,256]{3,2,1,0:T(8,128)} fusion(bf16[2,64,256,256]{3,2,1,0:T(8,128)(2,1)} %convolution_convert_fusion, bf16[1,256,256]{2,1,0:T(8,128)(2,1)S(1)} %copy-done.10), kind=kOutput, calls=%fused_computation.10 | convolution fusion | flops 4294967296 | bytes 50462720 | tf_op jit(solution)/shard_map/xeab,bc->xeac/dot_general | solution.py:108
  1292.0 115.2 %collective-permute-done = bf16[2,64,256,256]{2,3,1,0:T(8,128)(2,1)} collective-permute-done((bf16[2,64,256,256]{2,3,1,0:T(8,128)(2,1)}, bf16[2,64,256,256]{2,3,1,0:T(8,128)(2,1)}, u32[]{:S(2)}, u32[]{:S(2)}) %collective-permute-start) | collective-permute-done | bytes 16777248 | tf_op jit(solution)/shard_map/ppermute | solution.py:13
  1407.2 12.1 convolution_convert_fusion.1
  1419.4 21.4 %fusion.6 = f32[2,64,256,256]{3,2,1,0:T(8,128)} fusion(bf16[2,64,256,256]{3,2,1,0:T(8,128)(2,1)} %convolution_convert_fusion.1, bf16[1,256,256]{2,1,0:T(8,128)(2,1)S(1)} %copy-done.9), kind=kOutput, calls=%fused_computation.13 | convolution fusion | flops 4294967296 | bytes 50462720 | tf_op jit(solution)/shard_map/xeab,cb->xeac/dot_general | solution.py:105
  1440.8 23.6 %fusion.12 = bf16[2,64,1,256,256]{4,3,2,1,0:T(8,128)(2,1)} fusion(f32[2,64,256,256]{3,2,1,0:T(8,128)} %fusion.1, bf16[2,64,256,256]{3,2,1,0:T(8,128)(2,1)} %convolution_convert_fusion.1, bf16[256,256]{1,0:T(8,128)(2,1)S(1)} %collective-permute-done.3), kind=kOutput, calls=%fused_computation.23 | convolution fusion | flops 4311744512 | bytes 67239936 | tf_op jit(solution)/shard_map/xeab,bc->xeac/dot_general | solution.py:114
  1464.4 34.4 %fusion.15 = bf16[2,64,1,256,256]{4,3,2,1,0:T(8,128)(2,1)} fusion(bf16[2,64,256,256]{2,3,1,0:T(8,128)(2,1)} %collective-permute-done.1, f32[2,64,256,256]{3,2,1,0:T(8,128)} %fusion.6, f32[2,64,256,256]{3,2,1,0:T(8,128)} %fusion.3, bf16[256,256]{1,0:T(8,128)(2,1)S(1)} %collective-permute-done.2), kind=kOutput, calls=%fused_computation.24 | convolution fusion | flops 8623489024 | bytes 100794368 | tf_op jit(solution)/shard_map/xeab,bc->xeac/dot_general | solution.py:111
  (59 shorter events, 103.2 us)
Async XLA Ops:
  0.6 0.7 copy-start
  4.1 9.8 copy-start.11
  101.1 11.5 copy-start.2
  176.0 188.8 %all-to-all-start.1 = ((bf16[2,64,8,32,128]{4,3,1,0,2:T(8,128)(2,1)}), bf16[2,64,8,32,128]{4,3,1,0,2:T(8,128)(2,1)}, u32[]{:S(2)}, u32[]{:S(2)}) async-start(bf16[2,64,8,32,128]{4,3,1,0,2:T(8,128)(2,1)} %copy.63), calls=%async_computation.1 | async-start | bytes 16777216 | tf_op jit(solution)/shard_map/all_to_all | solution.py:63
  364.7 186.4 %all-to-all-start = ((bf16[2,64,8,32,128]{4,3,1,0,2:T(8,128)(2,1)}), bf16[2,64,8,32,128]{4,3,1,0,2:T(8,128)(2,1)}, u32[]{:S(2)}, u32[]{:S(2)}) async-start(bf16[2,64,8,32,128]{4,3,1,0,2:T(8,128)(2,1)} %copy.61), calls=%async_computation | async-start | bytes 16777216 | tf_op jit(solution)/shard_map/all_to_all | solution.py:62
  375.5 8.9 copy-start.3
  555.4 72.6 %copy-start.7 = (bf16[1,8,64,1,32,128]{5,4,2,0,1,3:T(8,128)(2,1)}, bf16[1,8,64,1,32,128]{5,4,2,0,1,3:T(8,128)(2,1)S(1)}, u32[]{:S(2)}) copy-start(bf16[1,8,64,1,32,128]{5,4,2,0,1,3:T(8,128)(2,1)S(1)} %get-tuple-element.19) | copy-start | bytes 12582916
  555.4 81.5 %copy-start.5 = (bf16[1,8,64,1,32,128]{5,4,2,0,1,3:T(8,128)(2,1)}, bf16[1,8,64,1,32,128]{5,4,2,0,1,3:T(8,128)(2,1)S(1)}, u32[]{:S(2)}) copy-start(bf16[1,8,64,1,32,128]{5,4,2,0,1,3:T(8,128)(2,1)S(1)} %get-tuple-element.20) | copy-start | bytes 12582916
  564.8 8.9 copy-start.6
  592.0 9.0 copy-start.4
  865.3 3.3 copy-start.8
  875.0 5.7 copy-start.12
  875.0 186.9 %all-to-all-start.2 = ((bf16[2,8,64,1,32,128]{5,4,2,3,0,1:T(8,128)(2,1)}), bf16[2,8,64,1,32,128]{5,4,2,3,0,1:T(8,128)(2,1)}, u32[]{:S(2)}, u32[]{:S(2)}) async-start(bf16[2,8,64,1,32,128]{5,4,2,3,0,1:T(8,128)(2,1)} %pad_maximum_fusion.1), calls=%async_computation.2 | async-start | bytes 16777216 | tf_op jit(solution)/shard_map/all_to_all | solution.py:89
  1199.3 33.3 %copy-start.10 = (bf16[1,256,256]{2,1,0:T(8,128)(2,1)S(1)}, bf16[1,256,256]{2,1,0:T(8,128)(2,1)}, u32[]{:S(2)}) copy-start(bf16[1,256,256]{2,1,0:T(8,128)(2,1)} %param.10) | copy-start | bytes 393220
  1199.3 35.3 %copy-start.9 = (bf16[1,256,256]{2,1,0:T(8,128)(2,1)S(1)}, bf16[1,256,256]{2,1,0:T(8,128)(2,1)}, u32[]{:S(2)}) copy-start(bf16[1,256,256]{2,1,0:T(8,128)(2,1)} %param.11) | copy-start | bytes 393220
  1220.6 186.7 %collective-permute-start = (bf16[2,64,256,256]{2,3,1,0:T(8,128)(2,1)}, bf16[2,64,256,256]{2,3,1,0:T(8,128)(2,1)}, u32[]{:S(2)}, u32[]{:S(2)}) collective-permute-start(bf16[2,64,256,256]{2,3,1,0:T(8,128)(2,1)} %copy.69), channel_id=1, source_target_pairs={{0,1},{1,2},{2,3},{4,5},{5,6},{6,7},{8,9},{9,10},{10,11},{12,13},{... | collective-permute-start | bytes 50331656 | tf_op jit(solution)/shard_map/ppermute | solution.py:13
  1226.7 237.8 %collective-permute-start.1 = (bf16[2,64,256,256]{2,3,1,0:T(8,128)(2,1)}, bf16[2,64,256,256]{2,3,1,0:T(8,128)(2,1)}, u32[]{:S(2)}, u32[]{:S(2)}) collective-permute-start(bf16[2,64,256,256]{2,3,1,0:T(8,128)(2,1)} %copy.69), channel_id=1, source_target_pairs={{1,0},{2,1},{3,2},{5,4},{6,5},{7,6},{9,8},{10,9},{11,10},{13,12},{... | collective-permute-start | bytes 50331656 | tf_op jit(solution)/shard_map/ppermute | solution.py:13
  1232.7 208.1 %collective-permute-start.3 = (bf16[256,256]{1,0:T(8,128)(2,1)S(1)}, bf16[256,256]{1,0:T(8,128)(2,1)S(1)}, u32[]{:S(2)}, u32[]{:S(2)}) collective-permute-start(bf16[256,256]{1,0:T(8,128)(2,1)S(1)} %bitcast.196), channel_id=1, source_target_pairs={{0,1},{1,2},{2,3},{4,5},{5,6},{6,7},{8,9},{9,10},{10,11},{12,13},{... | collective-permute-start | bytes 393224 | tf_op jit(solution)/shard_map/ppermute | solution.py:13
  1234.6 229.8 %collective-permute-start.2 = (bf16[256,256]{1,0:T(8,128)(2,1)S(1)}, bf16[256,256]{1,0:T(8,128)(2,1)S(1)}, u32[]{:S(2)}, u32[]{:S(2)}) collective-permute-start(bf16[256,256]{1,0:T(8,128)(2,1)S(1)} %bitcast.195), channel_id=1, source_target_pairs={{1,0},{2,1},{3,2},{5,4},{6,5},{7,6},{9,8},{10,9},{11,10},{13,12},{... | collective-permute-start | bytes 393224 | tf_op jit(solution)/shard_map/ppermute | solution.py:13
  1464.4 34.5 %copy-start.1 = (s32[1,512]{1,0:T(1,128)S(1)}, s32[1,512]{1,0:T(1,128)}, u32[]{:S(2)}) copy-start(s32[1,512]{1,0:T(1,128)} %param.13) | copy-start | bytes 6148
where the time goes:
time: 1510 us; the launch traced here: 1500 us
  waiting for transfers between devices  623 us (41%)
  matrix products  458 us (30%)
  local copies, waits for them, and re-layouts  352 us (23%)
  starting transfers between devices  34 us (2%)
  other arithmetic  32 us (2%)
    all_to_all x1, waiting for transfers between devices, per_device(): lax.all_to_all(polar_tiles, 'energy', split_axis=1, concat_axis=3, tiled=...  181 us
    all_to_all x1, waiting for transfers between devices, per_device(): lax.all_to_all(pack(greater), 'energy', split_axis=2, concat_axis=1, tile...  168 us
    all_to_all x1, waiting for transfers between devices, per_device(): lax.all_to_all(pack(lesser), 'energy', split_axis=2, concat_axis=1, tiled...  158 us
    ppermute x4, waiting for transfers between devices, passed_along(): lax.ppermute(value, axis, [(source, source + steps) for source in range(l...  115 us
    dot_general x8, matrix products, table_times(): return first + jnp.dot(parts[1], data, preferred_element_type=jnp.float32)  112 us
    reshape x2, local copies, waits for them, and re-layouts, pack(): tiled = source.reshape(2, local_energies, n_tiles, TILE)  77.6 us
    dot_general x8, matrix products, table_times(): first = jnp.dot(parts[0], data, preferred_element_type=jnp.float32)  72.3 us
    dot_general x2, matrix products, split_times(): return total + jnp.dot(parts[1], upper, preferred_element_type=jnp.float32)  47.5 us
  transfers between devices with their start and end apart: 7, of which 4 were waited for; matrix products, arithmetic and copies ran while one was open for 10% of the time, Pallas kernels for 0%

commit v1 on v0

--- a/solution.py
+++ b/solution.py
@@ -1,3 +1,4 @@
+import functools
 import jax
 import jax.numpy as jnp
 from jax import lax
@@ -5,6 +6,16 @@
 
 TILE = 128
 NNZ = 128
+
+
+def mix_fields_in(patch, dev_axis, dim_i, dim_no):
+    left_arr = jnp.stack(jnp.split(patch, lax.axis_size(dev_axis), axis=dim_i))
+    t1 = lax.all_to_all(left_arr, dev_axis, 0, 0)
+    state_now = jnp.concatenate(t1, axis=dim_no)
+    return state_now
+
+
+recover_tables_now = functools.partial(mix_fields_in, dev_axis="energy", dim_i=2, dim_no=1)
 
 
 def passed_along(value, axis, steps):
@@ -60,7 +71,7 @@
 
     lesser_got, greater_got = (
         lax.all_to_all(pack(lesser), "energy", split_axis=2, concat_axis=1, tiled=True),
-        lax.all_to_all(pack(greater), "energy", split_axis=2, concat_axis=1, tiled=True),
+        recover_tables_now(pack(greater)),
     )
     energies = local_energies * group_size
     columns = most_tiles * TILE

time: 1510 us -> 1470 us (0.974)
  waiting for transfers between devices: 623 us -> 588 us
    all_to_all x1, waiting for transfers between devices: 158 us -> 123 us  [per_device(): lax.all_to_all(pack(lesser), 'energy', split_axis=2, concat_axis=1, tiled...]
    unnamed x30 -> x39, local copies, waits for them, and re-layouts: 28.8 us -> 40.4 us
  transfers between devices with their start and end apart: 7 -> 7, of which waited for: 4 -> 4; matrix products, arithmetic and copies ran while one was open for 10% -> 13% of each run, Pallas kernels for 0% -> 0%
where the time goes in v1:
time: 1470 us; the launch traced here: 1460 us
  waiting for transfers between devices  588 us (40%)
  matrix products  456 us (31%)
  local copies, waits for them, and re-layouts  353 us (24%)
  starting transfers between devices  33.7 us (2%)
  other arithmetic  29.5 us (2%)
    all_to_all x1, waiting for transfers between devices, per_device(): lax.all_to_all(polar_tiles, 'energy', split_axis=1, concat_axis=3, tiled=...  181 us
    all_to_all x1, waiting for transfers between devices, mix_fields_in(): t1 = lax.all_to_all(left_arr, dev_axis, 0, 0)  169 us
    all_to_all x1, waiting for transfers between devices, per_device(): lax.all_to_all(pack(lesser), 'energy', split_axis=2, concat_axis=1, tiled...  123 us
    ppermute x4, waiting for transfers between devices, passed_along(): lax.ppermute(value, axis, [(source, source + steps) for source in range(l...  115 us
    dot_general x8, matrix products, table_times(): return first + jnp.dot(parts[1], data, preferred_element_type=jnp.float32)  110 us
    reshape x2, local copies, waits for them, and re-layouts, pack(): tiled = source.reshape(2, local_energies, n_tiles, TILE)  77.6 us
    dot_general x8, matrix products, table_times(): first = jnp.dot(parts[0], data, preferred_element_type=jnp.float32)  71.9 us
    dot_general x2, matrix products, split_times(): return total + jnp.dot(parts[1], upper, preferred_element_type=jnp.float32)  47.4 us
  transfers between devices with their start and end apart: 7, of which 4 were waited for; matrix products, arithmetic and copies ran while one was open for 13% of the time, Pallas kernels for 0%

profile of v1, /device:TPU:1, one launch (start us, length us, event | category | flops | bytes accessed | tf_op | source)
XLA Modules:
  0.0 1461.0 jit_solution(11968208874897855254)
XLA Ops:
  4.2 9.7 copy.124
  13.9 37.2 %copy.80 = bf16[2,64,512,128]{3,1,2,0:T(8,128)(2,1)S(1)} copy(bf16[2,64,512,128]{3,2,1,0:T(8,128)(2,1)S(1)} %bitcast.200) | data formatting | bytes 33554432 | tf_op jit(solution)/shard_map/reshape | solution.py:65
  51.1 9.7 copy.127
  60.8 40.3 %copy.82 = bf16[2,64,512,128]{3,1,2,0:T(8,128)(2,1)} copy(bf16[2,64,512,128]{3,2,1,0:T(8,128)(2,1)S(1)} %bitcast.201) | data formatting | bytes 33554432 | tf_op jit(solution)/shard_map/reshape | solution.py:65
  101.1 9.1 concatenate.17
  121.1 14.4 gather_fusion.1
  135.5 14.9 %gather_fusion.2 = bf16[256,2,64,128]{3,2,1,0:T(8,128)(2,1)} fusion(bf16[2,64,513,128]{3,1,2,0:T(8,128)(2,1)} %concatenate.18, s32[1024]{0:T(1024)S(1)} %pad_clamp_fusion), kind=kCustom, calls=%fused_computation.1.clone | custom fusion | bytes 16778240 | tf_op jit(solution)/shard_map/jit(_take)/gather | solution.py:69
  150.4 9.6 broadcast_select_fusion
  182.7 13.6 copy.81
  196.4 168.5 %all-to-all-done.1 = bf16[8,2,64,1,32,128]{5,4,2,3,1,0:T(8,128)(2,1)} async-done(((bf16[8,2,64,1,32,128]{5,4,2,3,1,0:T(8,128)(2,1)}), bf16[8,2,64,1,32,128]{5,4,2,3,1,0:T(8,128)(2,1)}, u32[]{:S(2)}, u32[]{:S(2)}) %all-to-all-start.1) | async-done | bytes 8388640 | tf_op jit(solution)/shard_map/all_to_all | solution.py:13
  374.3 9.0 fusion.29
  383.4 8.9 fusion.26
  392.3 8.9 fusion.36
  401.2 9.4 fusion.32
  410.5 8.9 fusion.34
  419.5 8.9 fusion.24
  428.4 122.9 %all-to-all-done = bf16[2,64,8,32,128]{4,3,1,0,2:T(8,128)(2,1)} async-done(((bf16[2,64,8,32,128]{4,3,1,0,2:T(8,128)(2,1)}), bf16[2,64,8,32,128]{4,3,1,0,2:T(8,128)(2,1)}, u32[]{:S(2)}, u32[]{:S(2)}) %all-to-all-start) | async-done | bytes 8388640 | tf_op jit(solution)/shard_map/all_to_all | solution.py:73
  555.6 9.1 fusion.48
  573.5 9.0 fusion.43
  582.5 9.2 fusion.38
  591.7 8.9 fusion.40
  600.5 9.0 fusion.46
  609.5 16.1 %add_subtract_fusion.1 = f32[512,4096]{1,0:T(8,128)S(1)} fusion(f32[512,4096]{1,0:T(8,128)} %fusion.29, f32[512,4096]{1,0:T(8,128)} %fusion.36, f32[512,4096]{1,0:T(8,128)} %fusion.34, bf16[64,8,32,128]{3,2,1,0:T(8,128)(2,1)} %bitcast.214), kind=kOutput, calls=%fused_computation.36 | convolution fusion | flops 2158493696 | bytes 37748736 | tf_op jit(solution)/shard_map/dot_general | solution.py:35
  625.6 15.7 %add_add_fusion.2 = f32[512,4096]{1,0:T(8,128)} fusion(f32[512,4096]{1,0:T(8,128)} %fusion.32, f32[512,4096]{1,0:T(8,128)} %fusion.26, f32[512,4096]{1,0:T(8,128)} %fusion.24, bf16[64,8,32,128]{3,2,1,0:T(8,128)(2,1)S(1)} %bitcast.210), kind=kOutput, calls=%fused_computation.34 | convolution fusion | flops 2158493696 | bytes 37748736 | tf_op jit(solution)/shard_map/dot_general | solution.py:35
  641.3 18.8 %add_add_fusion.3 = f32[512,4096]{1,0:T(8,128)} fusion(f32[512,4096]{1,0:T(8,128)} %fusion.43, f32[512,4096]{1,0:T(8,128)} %fusion.50, f32[512,4096]{1,0:T(8,128)} %fusion.48, bf16[64,8,32,128]{3,2,1,0:T(8,128)(2,1)} %bitcast.222), kind=kOutput, calls=%fused_computation.37 | convolution fusion | flops 2158493696 | bytes 37748736 | tf_op jit(solution)/shard_map/dot_general | solution.py:35
  660.0 23.2 %multiply_subtract_fusion = (f32[512,4096]{1,0:T(8,128)}, f32[512,4096]{1,0:T(8,128)}) fusion(f32[512,4096]{1,0:T(8,128)} %add_add_fusion.2, f32[512,4096]{1,0:T(8,128)} %add_add_fusion.3, f32[512,4096]{1,0:T(8,128)S(1)} %add_subtract_fusion.1, f32[512,4096]{1,0:T(8,128)} %fusion.46, bf16[64,8,32,128]{3,2,1,0:T(8,128)(2,1)S(1)} %bitcast.218, ...), kind=kOutput, calls=%fused_computation.33 | convolution fusion | flops 2171076608 | bytes 71303168 | tf_op jit(solution)/shard_map/dot_general | solution.py:35
  683.3 19.7 %fusion.85 = f32[512,8192]{1,0:T(8,128)} fusion(f32[512,4096]{1,0:T(8,128)} %get-tuple-element.16, f32[512,4096]{1,0:T(8,128)} %get-tuple-element.15), kind=kOutput, calls=%fused_computation.116 | convolution fusion | flops 4319870976 | bytes 33554432 | tf_op jit(solution)/shard_map/dot_general | solution.py:41
  702.9 19.9 %fusion.87 = f32[512,8192]{1,0:T(8,128)} fusion(f32[512,4096]{1,0:T(8,128)} %get-tuple-element.16, f32[512,4096]{1,0:T(8,128)} %get-tuple-element.15), kind=kOutput, calls=%fused_computation.117 | convolution fusion | flops 4315676672 | bytes 33554432 | tf_op jit(solution)/shard_map/dot_general | solution.py:40
  722.8 20.1 %fusion.94 = f32[512,8192]{1,0:T(8,128)} fusion(f32[512,4096]{1,0:T(8,128)} %get-tuple-element.16, f32[512,4096]{1,0:T(8,128)} %get-tuple-element.15), kind=kOutput, calls=%fused_computation.119 | convolution fusion | flops 4319870976 | bytes 33554432 | tf_op jit(solution)/shard_map/dot_general | solution.py:41
  742.9 20.5 %fusion.96 = f32[512,8192]{1,0:T(8,128)} fusion(f32[512,4096]{1,0:T(8,128)} %get-tuple-element.16, f32[512,4096]{1,0:T(8,128)} %get-tuple-element.15), kind=kOutput, calls=%fused_computation.120 | convolution fusion | flops 4315676672 | bytes 33554432 | tf_op jit(solution)/shard_map/dot_general | solution.py:40
  763.4 23.7 %add_add_fusion.1 = f32[512,8192]{1,0:T(8,128)} fusion(f32[512,8192]{1,0:T(8,128)} %fusion.87, f32[512,8192]{1,0:T(8,128)} %fusion.85, f32[512,4096]{1,0:T(8,128)} %get-tuple-element.16, f32[512,4096]{1,0:T(8,128)} %get-tuple-element.15), kind=kOutput, calls=%fused_computation.17 | convolution fusion | flops 4324851712 | bytes 67108864 | tf_op jit(solution)/shard_map/dot_general | solution.py:42
  787.1 23.7 %add_add_fusion = f32[512,8192]{1,0:T(8,128)} fusion(f32[512,8192]{1,0:T(8,128)} %fusion.96, f32[512,8192]{1,0:T(8,128)} %fusion.94, f32[512,4096]{1,0:T(8,128)} %get-tuple-element.16, f32[512,4096]{1,0:T(8,128)} %get-tuple-element.15), kind=kOutput, calls=%fused_computation.16 | convolution fusion | flops 4324851712 | bytes 67108864 | tf_op jit(solution)/shard_map/dot_general | solution.py:42
  810.9 12.7 fusion.22
  842.4 181.1 %all-to-all-done.2 = bf16[2,8,64,1,32,128]{5,4,2,3,0,1:T(8,128)(2,1)} async-done(((bf16[2,8,64,1,32,128]{5,4,2,3,0,1:T(8,128)(2,1)}), bf16[2,8,64,1,32,128]{5,4,2,3,0,1:T(8,128)(2,1)}, u32[]{:S(2)}, u32[]{:S(2)}) %all-to-all-start.2) | async-done | bytes 8388640 | tf_op jit(solution)/shard_map/all_to_all | solution.py:100
  1023.5 9.4 copy.93
  1032.9 12.2 copy.94
  1051.2 41.3 %scatter_fusion = bf16[2,64,513,128]{3,1,2,0:T(8,128)(2,1)} fusion(bf16[2,64,513,128]{3,1,2,0:T(8,128)(2,1)} %broadcast_in_dim.13, s32[256]{0:T(256)S(1)} %bitcast.227, bf16[256,2,64,128]{3,2,1,0:T(8,128)(2,1)} %copy.94), kind=kCustom, calls=%fused_computation.3 | custom fusion | bytes 25166848 | tf_op jit(solution)/shard_map/scatter | solution.py:47
  1100.7 36.2 %copy.95 = bf16[2,64,512,128]{3,2,1,0:T(8,128)(2,1)} copy(bf16[2,64,512,128]{3,1,2,0:T(8,128)(2,1)S(1)} %slice.58) | data formatting | bytes 33554432 | tf_op jit(solution)/shard_map/slice | solution.py:48
  1136.8 24.4 %reshape.178 = bf16[2,64,256,256]{3,2,1,0:T(8,128)(2,1)} reshape(bf16[2,64,512,128]{3,2,1,0:T(8,128)(2,1)} %copy.95) | data formatting | bytes 33554432 | tf_op jit(solution)/shard_map/reshape | solution.py:48
  1161.3 21.2 %copy.96 = bf16[2,64,256,256]{2,3,1,0:T(8,128)(2,1)} copy(bf16[2,64,256,256]{3,2,1,0:T(8,128)(2,1)} %reshape.178) | data formatting | bytes 33554432 | tf_op jit(solution)/shard_map/reshape | solution.py:48
  1198.7 12.4 convolution_convert_fusion
  1211.0 21.4 %fusion.1 = f32[2,64,256,256]{3,2,1,0:T(8,128)} fusion(bf16[2,64,256,256]{3,2,1,0:T(8,128)(2,1)} %convolution_convert_fusion, bf16[1,256,256]{2,1,0:T(8,128)(2,1)S(1)} %copy-done.10), kind=kOutput, calls=%fused_computation.8 | convolution fusion | flops 4294967296 | bytes 50462720 | tf_op jit(solution)/shard_map/xeab,cb->xeac/dot_general | solution.py:128
  1232.5 21.4 %fusion.3 = f32[2,64,256,256]{3,2,1,0:T(8,128)} fusion(bf16[2,64,256,256]{3,2,1,0:T(8,128)(2,1)} %convolution_convert_fusion, bf16[1,256,256]{2,1,0:T(8,128)(2,1)S(1)} %copy-done.11), kind=kOutput, calls=%fused_computation.10 | convolution fusion | flops 4294967296 | bytes 50462720 | tf_op jit(solution)/shard_map/xeab,bc->xeac/dot_general | solution.py:119
  1253.9 115.2 %collective-permute-done = bf16[2,64,256,256]{2,3,1,0:T(8,128)(2,1)} collective-permute-done((bf16[2,64,256,256]{2,3,1,0:T(8,128)(2,1)}, bf16[2,64,256,256]{2,3,1,0:T(8,128)(2,1)}, u32[]{:S(2)}, u32[]{:S(2)}) %collective-permute-start) | collective-permute-done | bytes 16777248 | tf_op jit(solution)/shard_map/ppermute | solution.py:24
  1369.1 12.1 convolution_convert_fusion.1
  1381.2 21.4 %fusion.6 = f32[2,64,256,256]{3,2,1,0:T(8,128)} fusion(bf16[2,64,256,256]{3,2,1,0:T(8,128)(2,1)} %convolution_convert_fusion.1, bf16[1,256,256]{2,1,0:T(8,128)(2,1)S(1)} %copy-done.10), kind=kOutput, calls=%fused_computation.13 | convolution fusion | flops 4294967296 | bytes 50462720 | tf_op jit(solution)/shard_map/xeab,cb->xeac/dot_general | solution.py:116
  1402.7 23.6 %fusion.12 = bf16[2,64,1,256,256]{4,3,2,1,0:T(8,128)(2,1)} fusion(f32[2,64,256,256]{3,2,1,0:T(8,128)} %fusion.1, bf16[2,64,256,256]{3,2,1,0:T(8,128)(2,1)} %convolution_convert_fusion.1, bf16[256,256]{1,0:T(8,128)(2,1)S(1)} %collective-permute-done.3), kind=kOutput, calls=%fused_computation.23 | convolution fusion | flops 4311744512 | bytes 67239936 | tf_op jit(solution)/shard_map/xeab,bc->xeac/dot_general | solution.py:125
  1426.3 34.5 %fusion.15 = bf16[2,64,1,256,256]{4,3,2,1,0:T(8,128)(2,1)} fusion(bf16[2,64,256,256]{2,3,1,0:T(8,128)(2,1)} %collective-permute-done.1, f32[2,64,256,256]{3,2,1,0:T(8,128)} %fusion.6, f32[2,64,256,256]{3,2,1,0:T(8,128)} %fusion.3, bf16[256,256]{1,0:T(8,128)(2,1)S(1)} %collective-permute-done.2), kind=kOutput, calls=%fused_computation.24 | convolution fusion | flops 8623489024 | bytes 100794368 | tf_op jit(solution)/shard_map/xeab,bc->xeac/dot_general | solution.py:122
  (69 shorter events, 108.8 us)
Async XLA Ops:
  0.6 0.7 copy-start
  4.1 9.8 copy-start.12
  101.1 11.5 copy-start.2
  176.1 188.8 %all-to-all-start.1 = ((bf16[8,2,64,1,32,128]{5,4,2,3,1,0:T(8,128)(2,1)}), bf16[8,2,64,1,32,128]{5,4,2,3,1,0:T(8,128)(2,1)}, u32[]{:S(2)}, u32[]{:S(2)}) async-start(bf16[8,2,64,1,32,128]{5,4,2,3,1,0:T(8,128)(2,1)} %fusion.71), calls=%async_computation.1 | async-start | bytes 16777216 | tf_op jit(solution)/shard_map/all_to_all | solution.py:13
  364.9 186.4 %all-to-all-start = ((bf16[2,64,8,32,128]{4,3,1,0,2:T(8,128)(2,1)}), bf16[2,64,8,32,128]{4,3,1,0,2:T(8,128)(2,1)}, u32[]{:S(2)}, u32[]{:S(2)}) async-start(bf16[2,64,8,32,128]{4,3,1,0,2:T(8,128)(2,1)} %copy.81), calls=%async_computation | async-start | bytes 16777216 | tf_op jit(solution)/shard_map/all_to_all | solution.py:73
  374.3 36.2 %copy-start.3 = (bf16[1,8,64,1,32,128]{5,4,2,3,0,1:T(8,128)(2,1)}, bf16[1,8,64,1,32,128]{5,4,2,3,0,1:T(8,128)(2,1)S(1)}, u32[]{:S(2)}) copy-start(bf16[1,8,64,1,32,128]{5,4,2,3,0,1:T(8,128)(2,1)S(1)} %get-tuple-element.17) | copy-start | bytes 12582916
  374.3 45.2 %copy-start.5 = (bf16[1,8,64,1,32,128]{5,4,2,3,0,1:T(8,128)(2,1)}, bf16[1,8,64,1,32,128]{5,4,2,3,0,1:T(8,128)(2,1)S(1)}, u32[]{:S(2)}) copy-start(bf16[1,8,64,1,32,128]{5,4,2,3,0,1:T(8,128)(2,1)S(1)} %get-tuple-element.18) | copy-start | bytes 12582916
  555.5 36.2 %copy-start.8 = (bf16[1,8,64,1,32,128]{5,4,2,0,1,3:T(8,128)(2,1)}, bf16[1,8,64,1,32,128]{5,4,2,0,1,3:T(8,128)(2,1)S(1)}, u32[]{:S(2)}) copy-start(bf16[1,8,64,1,32,128]{5,4,2,0,1,3:T(8,128)(2,1)S(1)} %get-tuple-element.27) | copy-start | bytes 12582916
  555.5 45.0 %copy-start.6 = (bf16[1,8,64,1,32,128]{5,4,2,0,1,3:T(8,128)(2,1)}, bf16[1,8,64,1,32,128]{5,4,2,0,1,3:T(8,128)(2,1)S(1)}, u32[]{:S(2)}) copy-start(bf16[1,8,64,1,32,128]{5,4,2,0,1,3:T(8,128)(2,1)S(1)} %get-tuple-element.28) | copy-start | bytes 12582916
  609.5 16.1 %copy-start.4 = (bf16[1,8,64,1,32,128]{5,4,2,3,0,1:T(8,128)(2,1)S(1)}, bf16[1,8,64,1,32,128]{5,4,2,3,0,1:T(8,128)(2,1)}, u32[]{:S(2)}) copy-start(bf16[1,8,64,1,32,128]{5,4,2,3,0,1:T(8,128)(2,1)} %copy-done.3) | copy-start | bytes 12582916
  641.3 18.8 %copy-start.7 = (bf16[1,8,64,1,32,128]{5,4,2,0,1,3:T(8,128)(2,1)S(1)}, bf16[1,8,64,1,32,128]{5,4,2,0,1,3:T(8,128)(2,1)}, u32[]{:S(2)}) copy-start(bf16[1,8,64,1,32,128]{5,4,2,0,1,3:T(8,128)(2,1)} %copy-done.6) | copy-start | bytes 12582916
  826.9 3.3 copy-start.9
  836.5 5.8 copy-start.13
  836.5 187.0 %all-to-all-start.2 = ((bf16[2,8,64,1,32,128]{5,4,2,3,0,1:T(8,128)(2,1)}), bf16[2,8,64,1,32,128]{5,4,2,3,0,1:T(8,128)(2,1)}, u32[]{:S(2)}, u32[]{:S(2)}) async-start(bf16[2,8,64,1,32,128]{5,4,2,3,0,1:T(8,128)(2,1)} %pad_maximum_fusion.1), calls=%async_computation.2 | async-start | bytes 16777216 | tf_op jit(solution)/shard_map/all_to_all | solution.py:100
  1161.3 33.1 %copy-start.11 = (bf16[1,256,256]{2,1,0:T(8,128)(2,1)S(1)}, bf16[1,256,256]{2,1,0:T(8,128)(2,1)}, u32[]{:S(2)}) copy-start(bf16[1,256,256]{2,1,0:T(8,128)(2,1)} %param.10) | copy-start | bytes 393220
  1161.3 35.0 %copy-start.10 = (bf16[1,256,256]{2,1,0:T(8,128)(2,1)S(1)}, bf16[1,256,256]{2,1,0:T(8,128)(2,1)}, u32[]{:S(2)}) copy-start(bf16[1,256,256]{2,1,0:T(8,128)(2,1)} %param.11) | copy-start | bytes 393220
  1182.5 186.7 %collective-permute-start = (bf16[2,64,256,256]{2,3,1,0:T(8,128)(2,1)}, bf16[2,64,256,256]{2,3,1,0:T(8,128)(2,1)}, u32[]{:S(2)}, u32[]{:S(2)}) collective-permute-start(bf16[2,64,256,256]{2,3,1,0:T(8,128)(2,1)} %copy.96), channel_id=1, source_target_pairs={{0,1},{1,2},{2,3},{4,5},{5,6},{6,7},{8,9},{9,10},{10,11},{12,13},{... | collective-permute-start | bytes 50331656 | tf_op jit(solution)/shard_map/ppermute | solution.py:24
  1188.6 237.7 %collective-permute-start.1 = (bf16[2,64,256,256]{2,3,1,0:T(8,128)(2,1)}, bf16[2,64,256,256]{2,3,1,0:T(8,128)(2,1)}, u32[]{:S(2)}, u32[]{:S(2)}) collective-permute-start(bf16[2,64,256,256]{2,3,1,0:T(8,128)(2,1)} %copy.96), channel_id=1, source_target_pairs={{1,0},{2,1},{3,2},{5,4},{6,5},{7,6},{9,8},{10,9},{11,10},{13,12},{... | collective-permute-start | bytes 50331656 | tf_op jit(solution)/shard_map/ppermute | solution.py:24
  1194.3 208.3 %collective-permute-start.3 = (bf16[256,256]{1,0:T(8,128)(2,1)S(1)}, bf16[256,256]{1,0:T(8,128)(2,1)S(1)}, u32[]{:S(2)}, u32[]{:S(2)}) collective-permute-start(bf16[256,256]{1,0:T(8,128)(2,1)S(1)} %bitcast.226), channel_id=1, source_target_pairs={{0,1},{1,2},{2,3},{4,5},{5,6},{6,7},{8,9},{9,10},{10,11},{12,13},{... | collective-permute-start | bytes 393224 | tf_op jit(solution)/shard_map/ppermute | solution.py:24
  1196.3 230.0 %collective-permute-start.2 = (bf16[256,256]{1,0:T(8,128)(2,1)S(1)}, bf16[256,256]{1,0:T(8,128)(2,1)S(1)}, u32[]{:S(2)}, u32[]{:S(2)}) collective-permute-start(bf16[256,256]{1,0:T(8,128)(2,1)S(1)} %bitcast.225), channel_id=1, source_target_pairs={{1,0},{2,1},{3,2},{5,4},{6,5},{7,6},{9,8},{10,9},{11,10},{13,12},{... | collective-permute-start | bytes 393224 | tf_op jit(solution)/shard_map/ppermute | solution.py:24
  1426.3 34.5 %copy-start.1 = (s32[1,512]{1,0:T(1,128)S(1)}, s32[1,512]{1,0:T(1,128)}, u32[]{:S(2)}) copy-start(s32[1,512]{1,0:T(1,128)} %param.13) | copy-start | bytes 6148
